TPU v7x, 512 devices: a whole 4x4x16 slice. The times are simulated.
512 devices in a mesh: space: 16 (over x_hi, y, core), tm: 32 (over z, x_lo).
Axes of the slice: x: 4 (x_hi: 2, x_lo: 2; x = x_hi * 2 + x_lo), y: 4, z: 16, core: 2. Of those that a mesh axis runs over, the one named last changes fastest.
Arguments:
- space_factor: bfloat16 [64, 65536], P('tm', 'space'), may hold values from -2.5 to 2.5
- time_factor: bfloat16 [64, 8192], P('space', 'tm'), may hold values from -2.5 to 2.5
- initial_state: float32 [65536], P('space'), may hold values from -6 to 6
- link: int32 [65536], P('space'), may hold values from 1 to 4
- conductivity: float32 [65536], P('space'), may hold values from 0.2 to 2
- mass: float32 [65536], P('space'), may hold values from 0.5 to 2
- reaction: float32 [65536], P('space'), may hold values from 0.05 to 0.4
- source: bfloat16 [65536, 8192], P('space', 'tm'), may hold values from -6 to 6
Outputs:
- grad_space: float32 [64, 65536], P('tm', 'space')
- grad_time: float32 [64, 8192], P('space', 'tm')
Inputs may be any that keep to these rules, and one draw needn't show every extreme that they name: Element i joins node i and node i + link[i]; where that node lies past the last node, the element ties node i to a zero value.
All inputs are finite; a program needn't handle non-finite values.
Results may differ from a plain program's by a relative error of at most 0.00055.
Values may be sent and summed in bfloat16 or wider, within the bound.
No kernel may reach another device: no remote copies, remote signals or barrier semaphores. Data moves between devices by JAX's collectives and lax.ppermute only.
A program may use at most 64 MiB of HBM per device.

v0:
```python
import math

import jax
import jax.numpy as jnp
from jax import lax
from jax.sharding import PartitionSpec as P

W = 4


def from_behind(array, axis, by):
    length = lax.axis_size(axis)
    pairs = [(i, i + by) for i in range(length) if 0 <= i + by < length]
    return lax.ppermute(array, axis, pairs)


def padded_2(array, sides, width):
    for axis, dim in sides:
        size, length = (lax.axis_size(axis), array.shape[dim])
        up = [(i, (i + 1) % size) for i in range(size - 1)]
        down = [(j, i) for i, j in up]
        last = lax.slice_in_dim(array, length - width, length, axis=dim)
        initial = lax.slice_in_dim(array, 0, width, axis=dim)
        before = lax.ppermute(last, axis, up)
        after = lax.ppermute(initial, axis, down)
        array = jnp.concatenate([before, array, after], axis=dim)
    return array


def diffuse(padded, rates_padded, count):
    total = None
    for offset in range(1, W + 1):
        own_rate = rates_padded[offset - 1, W : W + count][:, None]
        came_rate = rates_padded[offset - 1, W - offset : W - offset + count][:, None]
        centre = padded[W : W + count]
        term = own_rate * (centre - padded[W + offset : W + offset + count]) - came_rate * (
            padded[W - offset : W - offset + count] - centre
        )
        total = term if total is None else total + term
    return total


def contract(left, right):
    return lax.dot_general(
        left, right, (((0,), (0,)), ((), ())), preferred_element_type=jnp.float32
    )


def body(space_factor, time_factor, initial_state, link, conductivity, mass, reaction, source):
    node_count = space_factor.shape[1]
    step_count = time_factor.shape[1]
    time_full = lax.all_gather(time_factor, "space", axis=0, tiled=True)
    space_full = None
    carried = None
    space_full = lax.all_gather(space_factor, "tm", axis=0, tiled=True)
    state = contract(space_full, time_full)
    carried = from_behind(state[:, -1], "tm", 1)
    leading = lax.axis_index("tm") == 0
    prior_col = jnp.where(leading, initial_state, carried)
    earlier = jnp.concatenate([prior_col[:, None], state[:, :-1]], axis=1)
    offsets = jnp.arange(1, W + 1, dtype=jnp.int32)[:, None]
    rates = jnp.where(link[None, :] == offsets, conductivity[None, :], 0.0)
    below_rates = from_behind(rates[:, node_count - W :], "space", 1)
    rates_padded = jnp.concatenate([below_rates, rates], axis=1)
    padded = padded_2(state, (("space", 0),), W)
    mass_col = mass[:, None]
    react_col = reaction[:, None]
    residual = (
        mass_col * (state - earlier)
        + diffuse(padded, rates_padded, node_count)
        + react_col * state * state * state
        - source.astype(jnp.float32)
    )
    following = from_behind(residual[:, 0], "tm", -1)
    later = jnp.concatenate([residual[:, 1:], following[:, None]], axis=1)
    padded_residual = padded_2(residual, (("space", 0),), W)
    descent = (
        mass_col * (residual - later)
        + diffuse(padded_residual, rates_padded, node_count)
        + 3.0 * react_col * state * state * residual
    )
    descent_b = descent.astype(jnp.bfloat16)
    steps_all = step_count * lax.axis_size("tm")
    nodes_all = node_count * lax.axis_size("space")
    picked = time_full
    grad_space = lax.psum_scatter(
        lax.dot_general(
            picked, descent_b, (((1,), (1,)), ((), ())), preferred_element_type=jnp.float32
        ),
        "tm",
        scatter_dimension=0,
        tiled=True,
    ) / math.sqrt(steps_all)
    picked = space_full
    node_sums = lax.psum_scatter(
        jnp.dot(picked, descent_b, preferred_element_type=jnp.float32),
        "space",
        scatter_dimension=0,
        tiled=True,
    )
    grad_time = node_sums / math.sqrt(nodes_all)
    return (grad_space, grad_time)


def solution(mesh):
    in_specs = (
        P("tm", "space"),
        P("space", "tm"),
        P("space"),
        P("space"),
        P("space"),
        P("space"),
        P("space"),
        P("space", "tm"),
    )
    out_specs = (P("tm", "space"), P("space", "tm"))
    return jax.shard_map(body, mesh=mesh, in_specs=in_specs, out_specs=out_specs, check_vma=False)
```

profile of v0, /device:TPU:24, one launch (start us, length us, event | category | flops | bytes accessed | tf_op | source)
XLA Modules:
  0.0 598.9 jit_solution(14351321692977313970)
XLA Ops:
  7.2 0.8 compare_select_fusion
  8.1 1.9 collective-permute-start.2
  10.0 72.3 %all-gather = bf16[32,2,4096]{2,1,0:T(2,128)(2,1)S(1)} all-gather(bf16[1,2,4096]{2,1,0:T(2,128)(2,1)} %bitcast.44), channel_id=1, replica_groups=mesh['space'=16,'tm'=32] {'tm'}, dimensions={0}, use_global_device_ids=true | all-gather | bytes 540672 | tf_op jit(solution)/shard_map/all_gather | solution.py:55
  82.5 18.7 %all-gather.1 = bf16[16,4,256]{2,1,0:T(4,128)(2,1)S(1)} all-gather(bf16[1,4,256]{2,1,0:T(4,128)(2,1)} %bitcast.45), channel_id=1, replica_groups=mesh['space'=16,'tm'=32] {'space'}, dimensions={0}, use_global_device_ids=true | all-gather | bytes 34816 | tf_op jit(solution)/shard_map/all_gather | solution.py:52
  102.0 3.3 collective-permute-start.1
  105.4 1.9 collective-permute-start.3
  107.3 1.2 slice_reduce_fusion.1
  108.5 1.3 collective-permute-start
  110.0 1.2 collective-permute-done
  111.9 22.1 %fusion.1 = f32[4096,256]{1,0:T(8,128)S(1)} fusion(f32[4096,256]{1,0:T(8,128)} %copy-done, f32[4,256]{1,0:T(4,128)S(1)} %collective-permute-done.3, f32[4,256]{1,0:T(4,128)S(1)} %collective-permute-done.1, f32[4096,255]{1,0:T(8,128)} %bitcast.25, f32[4096,1]{1,0:T(8,128)S(1)} %copy.12, bf16[4096,256]{1,0:T(8,128)(2,1)} %param.15, f32[4096]{0:T(1024)S(1)} %copy-done.2, ...), kind=kLoop, calls=%fused_computation.16 | loop fusion | flops 42991616 | bytes 14852096 | tf_op jit(solution)/shard_map/sub | solution.py:69
  134.6 1.3 collective-permute-start.4
  135.9 3.1 collective-permute-start.5
  139.0 5.1 collective-permute-start.6
  144.1 3.1 slice.177
  147.3 2.0 copy.13
  149.2 21.7 %fusion.4 = bf16[4096,256]{1,0:T(8,128)(2,1)S(1)} fusion(f32[4096,256]{1,0:T(8,128)} %copy-done.1, f32[4096,256]{1,0:T(8,128)} %copy-done, f32[4,256]{1,0:T(4,128)S(1)} %collective-permute-done.6, f32[4,256]{1,0:T(4,128)S(1)} %collective-permute-done.5, f32[4096,1]{1,0:T(8,128)} %copy.13, f32[4096,255]{1,0:T(8,128)} %slice.177, ...), kind=kLoop, calls=%fused_computation.19 | loop fusion | flops 41943040 | bytes 14852096 | tf_op jit(solution)/shard_map/convert_element_type | solution.py:82
  170.9 1.1 convolution_bitcast_fusion.1
  172.1 1.8 convolution_bitcast_fusion
  173.9 1.3 dynamic-slice.2
  175.2 1.3 dynamic-slice
  177.7 138.8 %all-reduce.7.cloned.1.call-done = f32[64,256]{1,0:T(8,128)} async-done(((f32[64,256]{1,0:T(8,128)}), f32[64,256]{1,0:T(8,128)}) %all-reduce.7.cloned.1.call-update) | async-done | bytes 65552
  316.6 1.3 dynamic-slice_multiply_fusion.1
  317.9 272.6 %all-reduce.5.cloned.1.call-done = f32[64,4096]{1,0:T(8,128)} async-done(((f32[64,4096]{1,0:T(8,128)}), f32[64,4096]{1,0:T(8,128)}) %all-reduce.5.cloned.1.call-update) | async-done | bytes 1048592
  590.5 1.5 dynamic-slice_multiply_fusion
  (32 shorter events, 2.7 us)
Async XLA Ops:
  7.2 309.4 %all-reduce.7.cloned.1.call-start = ((), (), s32[]{:S(2)}) async-start(), calls=%async_computation.1 | async-start | bytes 131072
  8.1 101.7 %collective-permute-start.2 = (f32[4,4]{1,0:T(4,128)S(1)}, f32[4,4]{1,0:T(4,128)S(1)}, u32[]{:S(2)}, u32[]{:S(2)}) collective-permute-start(f32[4,4]{1,0:T(4,128)S(1)} %slice.162), channel_id=1, source_target_pairs={{0,32},{32,64},{64,96},{96,128},{128,160},{160,192},{192,224},{224... | collective-permute-start | bytes 200 | tf_op jit(solution)/shard_map/ppermute | solution.py:14
  82.3 28.9 %copy-start.4 = (f32[4096]{0:T(1024)S(1)}, f32[4096]{0:T(1024)}, u32[]{:S(2)}) copy-start(f32[4096]{0:T(1024)} %param.10) | copy-start | bytes 49156
  101.2 10.6 %copy-start.2 = (f32[4096]{0:T(1024)S(1)}, f32[4096]{0:T(1024)}, u32[]{:S(2)}) copy-start(f32[4096]{0:T(1024)} %param.14) | copy-start | bytes 49156
  101.3 10.6 %copy-start.3 = (f32[4096]{0:T(1024)S(1)}, f32[4096]{0:T(1024)}, u32[]{:S(2)}) copy-start(f32[4096]{0:T(1024)} %param.13) | copy-start | bytes 49156
  102.0 5.3 copy-start
  102.0 9.8 %collective-permute-start.1 = (f32[4,256]{1,0:T(4,128)S(1)}, f32[4,256]{1,0:T(4,128)S(1)}, u32[]{:S(2)}, u32[]{:S(2)}) collective-permute-start(f32[4,256]{1,0:T(4,128)S(1)} %get-tuple-element.4), channel_id=1, source_target_pairs={{32,0},{64,32},{96,64},{128,96},{160,128},{192,160},{224,192},{256... | collective-permute-start | bytes 12296 | tf_op jit(solution)/shard_map/ppermute | solution.py:25
  105.4 6.5 %collective-permute-start.3 = (f32[4,256]{1,0:T(4,128)S(1)}, f32[4,256]{1,0:T(4,128)S(1)}, u32[]{:S(2)}, u32[]{:S(2)}) collective-permute-start(f32[4,256]{1,0:T(4,128)S(1)} %get-tuple-element.5), channel_id=1, source_target_pairs={{0,32},{32,64},{64,96},{96,128},{128,160},{160,192},{192,224},{224... | collective-permute-start | bytes 12296 | tf_op jit(solution)/shard_map/ppermute | solution.py:24
  108.5 2.7 collective-permute-start
  134.0 13.2 %copy-start.1 = (f32[4096,256]{1,0:T(8,128)}, f32[4096,256]{1,0:T(8,128)S(1)}, u32[]{:S(2)}) copy-start(f32[4096,256]{1,0:T(8,128)S(1)} %fusion.1) | copy-start | bytes 12582916
  134.6 12.6 %collective-permute-start.4 = (f32[4096]{0:T(1024)S(1)}, f32[4096]{0:T(1024)S(1)}, u32[]{:S(2)}, u32[]{:S(2)}) collective-permute-start(f32[4096]{0:T(1024)S(1)} %slice_reduce_fusion), channel_id=1, source_target_pairs={{1,0},{2,1},{3,2},{4,3},{5,4},{6,5},{7,6},{8,7},{9,8},{10,9},{11,1... | collective-permute-start | bytes 49160 | tf_op jit(solution)/shard_map/ppermute | solution.py:14
  135.9 13.3 %collective-permute-start.5 = (f32[4,256]{1,0:T(4,128)S(1)}, f32[4,256]{1,0:T(4,128)S(1)}, u32[]{:S(2)}, u32[]{:S(2)}) collective-permute-start(f32[4,256]{1,0:T(4,128)S(1)} %get-tuple-element.2), channel_id=1, source_target_pairs={{32,0},{64,32},{96,64},{128,96},{160,128},{192,160},{224,192},{256... | collective-permute-start | bytes 12296 | tf_op jit(solution)/shard_map/ppermute | solution.py:25
  139.0 10.2 %collective-permute-start.6 = (f32[4,256]{1,0:T(4,128)S(1)}, f32[4,256]{1,0:T(4,128)S(1)}, u32[]{:S(2)}, u32[]{:S(2)}) collective-permute-start(f32[4,256]{1,0:T(4,128)S(1)} %get-tuple-element.3), channel_id=1, source_target_pairs={{0,32},{32,64},{64,96},{96,128},{128,160},{160,192},{192,224},{224... | collective-permute-start | bytes 12296 | tf_op jit(solution)/shard_map/ppermute | solution.py:24
  172.0 418.5 %all-reduce.5.cloned.1.call-start = ((), (), s32[]{:S(2)}) async-start(), calls=%async_computation | async-start | bytes 2097152
Sparse Core Ops, SparseCore 0:
  172.2 144.3 all-reduce.6
  319.5 270.9 all-reduce.4
where the time goes:
time: 600 us; the launch traced here: 599 us
  waiting for transfers between devices  413 us (69%)
  blocking collectives  91 us (15%)
  other arithmetic  47.6 us (8%)
  starting transfers between devices  18 us (3%)
  between operations  15.6 us (3%)
  local copies, waits for them, and re-layouts  10.4 us (2%)
    unnamed x4, waiting for transfers between devices  412 us
    all_gather x1, blocking collectives, body(): space_full = lax.all_gather(space_factor, 'tm', axis=0, tiled=True)  72.3 us
    sub x1, other arithmetic, body(): mass_col * (state - earlier) + diffuse(padded, rates_padded, node_count)  22.1 us
    convert_element_type x1, other arithmetic, body(): descent_b = descent.astype(jnp.bfloat16)  21.7 us
    all_gather x1, blocking collectives, body(): time_full = lax.all_gather(time_factor, 'space', axis=0, tiled=True)  18.7 us
  transfers between devices with their start and end apart: 9, of which 3 were waited for; matrix products, arithmetic and copies ran while one was open for 2% of the time, Pallas kernels for 0%

commit v1 on v0

v1 whole, which is shorter than its diff:
```python
import functools
import math

import jax
import jax.numpy as jnp
from jax import lax
from jax.experimental import pallas as pl
from jax.experimental.pallas import tpu as pltpu
from jax.sharding import PartitionSpec as P


W = 4
PAD = 128
TILE = 256
UNROLL = 2
BF = jnp.bfloat16
F32 = jnp.float32


def dot(a, b, ca, cb):
    return lax.dot_general(a, b, (((ca,), (cb,)), ((), ())), preferred_element_type=F32)


def halves(x):
    hi = x.astype(BF)
    return hi, (x - hi.astype(F32)).astype(BF)


def pack_kernel(
    s_lo, s_hi, cond_lo, cond_hi, link_lo, link_hi, mass_lo, mass_hi, reac_lo, reac_hi,
    init_lo, init_hi, src_lo, src_hi, src_first, time_ref, up_ref, down_ref, prev_ref, next_ref,
):
    for ref, parts, src in (
        (down_ref, (s_lo, cond_lo, link_lo, mass_lo, reac_lo, init_lo), src_lo[0:4, :]),
        (up_ref, (s_hi, cond_hi, link_hi, mass_hi, reac_hi, init_hi), src_hi[12:16, :]),
    ):
        rows = [p[...].astype(F32) for p in parts]
        rows.append(jnp.zeros((1, PAD), F32))
        src = src.astype(F32)
        ref[...] = jnp.concatenate(rows + [src[:, 0:PAD], src[:, PAD:]], axis=0)

    nodes = src_first.shape[0]
    steps = time_ref.shape[1]
    row = lax.broadcasted_iota(jnp.int32, (16, steps), 0)
    col = lax.broadcasted_iota(jnp.int32, (16, steps), 1)
    pick = jnp.where(((row == 0) & (col == 0)) | ((row == 1) & (col == steps - 1)), 1.0, 0.0).astype(BF)
    column = dot(pick[:, 0:PAD], src_first[...], 1, 1)
    for c in range(nodes // PAD):
        prev_ref[c : c + 1, :] = column[0:1, c * PAD : (c + 1) * PAD]
    ends = dot(pick, time_ref[...], 1, 1)[0:8]
    ends = jnp.concatenate([ends, jnp.zeros((8, PAD - ends.shape[1]), F32)], axis=1)
    prev_ref[nodes // PAD :, :] = ends
    next_ref[...] = ends


def encode_kernel(own_ref, came_ref, out_ref, flat_ref):
    rows, nodes = own_ref.shape
    n_row = nodes // PAD
    n_z = out_ref.shape[0]
    own_rank = rows // n_z
    body = own_rank * n_row
    for g in range(rows // 8):
        v = own_ref[8 * g : 8 * g + 8, :] + came_ref[8 * g : 8 * g + 8, :]
        top = jnp.max(jnp.abs(v), axis=1, keepdims=True)
        power = jnp.ceil(jnp.log2(jnp.maximum(top, 1e-30)) + 0.01) - 15.0
        q = jnp.floor(v * jnp.exp2(-power) + 0.5)
        for c in range(n_row):
            flat_ref[pl.ds(8 * g * n_row + c, 8, stride=n_row), :] = q[:, c * PAD : (c + 1) * PAD]
        for b in range(8):
            z, at = divmod(8 * g + b, own_rank)
            flat_ref[rows * n_row + 8 * z + at : rows * n_row + 8 * z + at + 1, :] = jnp.broadcast_to(
                power[b : b + 1], (1, PAD)
            )
    for z in range(n_z):
        out_ref[z, 0:body, :] = flat_ref[z * body : (z + 1) * body, :].astype(jnp.int32).astype(jnp.int16)
        tail = flat_ref[rows * n_row + 8 * z : rows * n_row + 8 * z + 8, :]
        tail = jnp.where(lax.broadcasted_iota(jnp.int32, (8, PAD), 0) < own_rank, tail, 0.0)
        out_ref[z, body : body + 8, :] = tail.astype(jnp.int32).astype(jnp.int16)


def decode_kernel(factor, in_ref, out_ref):
    n_z = in_ref.shape[0]
    own_rank, nodes = out_ref.shape
    n_row = nodes // PAD
    body = own_rank * n_row
    total = jnp.zeros((body, PAD), F32)
    for z in range(n_z):
        step = jnp.exp2(in_ref[z, body : body + 8, :].astype(jnp.int32).astype(F32))
        q = in_ref[z, 0:body, :].astype(jnp.int32).astype(F32)
        total = total + jnp.concatenate(
            [q[b * n_row : (b + 1) * n_row] * step[b : b + 1] for b in range(own_rank)], axis=0
        )
    total = total * factor
    for b in range(own_rank):
        for c in range(n_row):
            out_ref[b : b + 1, c * PAD : (c + 1) * PAD] = total[b * n_row + c : b * n_row + c + 1]


def compute_kernel(
    flag_ref, sown_ref, soth_ref, tt_ref, qt_ref, tlast_ref,
    below_ref, above_ref, cond_ref, link_ref, mass_ref, reac_ref, init_ref, srcn_ref, src_ref, edge_ref,
    gs_own_ref, gs_oth_ref, gt_ref,
    w_ref, g_ref, coef_ref, band_ref, row_ref, sn_ref, rn_ref, y_ref, acc1_ref, acc2_ref, acc3_ref,
):
    ext = coef_ref.shape[1]
    nodes = ext - 2 * PAD
    rank = tlast_ref.shape[0]
    half = rank // 2
    steps = src_ref.shape[1]
    main = pl.ds(PAD, nodes)
    right = pl.ds(PAD + nodes, PAD)

    for r, ref in enumerate((cond_ref, link_ref, mass_ref, reac_ref, init_ref)):
        coef_ref[r : r + 1, 0:PAD] = below_ref[2 + r : 3 + r, :]
        coef_ref[r : r + 1, main] = ref[...].astype(F32)
        coef_ref[r : r + 1, right] = above_ref[2 + r : 3 + r, :]

    cond = coef_ref[0:1, :]
    link = coef_ref[1:2, :]
    mass = coef_ref[2:3, :]
    diag = mass + cond
    tall = (8, ext)
    for d in range(1, W + 1):
        up = jnp.where(link == float(d), cond, 0.0)
        down = pltpu.roll(up, d, 1)
        band_ref[8 * d : 8 * d + 8, :] = jnp.broadcast_to(up, tall)
        band_ref[8 * (W + d) : 8 * (W + d) + 8, :] = jnp.broadcast_to(down, tall)
        diag = diag + down
    band_ref[0:8, :] = jnp.broadcast_to(diag, tall)
    band_ref[8 * (2 * W + 1) : 8 * (2 * W + 2), :] = jnp.broadcast_to(mass, tall)
    start = flag_ref[0]
    coef_ref[4:5, :] = coef_ref[4:5, :] * mass * start

    n_tile = ext // PAD

    def place(c):
        k, h = (n_tile // 2 - 1, int(c > 0)) if c in (0, n_tile - 1) else divmod(c - 1, 2)
        return k, slice(h * PAD, (h + 1) * PAD)

    for c in range(n_tile):
        k, sl = place(c)
        row_ref[k, 0:2, sl] = coef_ref[3:5, c * PAD : (c + 1) * PAD]

    lane1 = lax.broadcasted_iota(jnp.int32, (8, PAD), 1)

    def banded(tiles, keep):
        fwd = [[pltpu.roll(x, PAD - d, 1) for d in range(1, W + 1)] for x in tiles]
        bwd = [[pltpu.roll(x, d, 1) for d in range(1, W + 1)] for x in tiles]
        for c in range(n_tile):
            sl = slice(c * PAD, (c + 1) * PAD)
            nxt, prv = min(c + 1, n_tile - 1), max(c - 1, 0)
            total = band_ref[0:8, sl] * tiles[c]
            for d in range(1, W + 1):
                ahead = jnp.where(lane1 >= PAD - d, fwd[nxt][d - 1], fwd[c][d - 1])
                back = jnp.where(lane1 < d, bwd[prv][d - 1], bwd[c][d - 1])
                total = total - band_ref[8 * d : 8 * d + 8, sl] * ahead
                total = total - band_ref[8 * (W + d) : 8 * (W + d) + 8, sl] * back
            keep(c, total, tiles[c])

    for base, ref in ((0, sown_ref), (half, soth_ref)):
        def fill(i, _, base=base, ref=ref):
            at = pl.multiple_of(i * 16, 16)
            to = pl.multiple_of(base + i * 16, 16)
            s_b = ref[pl.ds(at, 16), :]
            s_f = s_b.astype(F32)
            got = []
            for h in range(2):
                mine = {}

                def keep(c, value, v, mine=mine):
                    m = band_ref[8 * (2 * W + 1) : 8 * (2 * W + 2), c * PAD : (c + 1) * PAD]
                    if c in (0, n_tile - 1):
                        value = jnp.where(m > 0.0, value, 0.0)
                    mine[c] = (value, m * v)

                banded([s_f[8 * h : 8 * h + 8, c * PAD : (c + 1) * PAD] for c in range(n_tile)], keep)
                got.append(mine)
            for c in range(n_tile):
                k, sl = place(c)
                w_ref[k, pl.ds(to + 4 * rank, 16), sl] = s_b[:, c * PAD : (c + 1) * PAD]
                a_hi, a_lo = halves(jnp.concatenate([got[0][c][0], got[1][c][0]], axis=0))
                b_hi, b_lo = halves(jnp.concatenate([got[0][c][1], got[1][c][1]], axis=0))
                w_ref[k, pl.ds(to, 16), sl] = a_hi
                w_ref[k, pl.ds(to + rank, 16), sl] = b_hi
                w_ref[k, pl.ds(to + 2 * rank, 16), sl] = a_lo
                w_ref[k, pl.ds(to + 3 * rank, 16), sl] = b_lo
            return 0

        lax.fori_loop(0, half // 16, fill, 0)

    lane = lax.broadcasted_iota(jnp.int32, (rank, steps), 1)
    row8 = lax.broadcasted_iota(jnp.int32, (8, TILE), 0)

    def residual(w, reac, init, src, src_next):
        lin = dot(qt_ref[...], w[0 : 4 * rank], 1, 0)
        u = dot(qt_ref[:, 0:rank], w[4 * rank : 5 * rank], 1, 0)
        ru2 = reac * (u * u)
        full = lin + ru2 * u
        res = full[0:steps] - src
        res = jnp.concatenate([res[0:8] - jnp.where(row8 == 0, init, 0.0), res[8:]], axis=0)
        after = full[steps : steps + 1] - src_next
        return res, after, ru2[0:steps]

    acc1_ref[...] = jnp.zeros_like(acc1_ref)
    acc2_ref[...] = jnp.zeros_like(acc2_ref)
    acc3_ref[...] = jnp.zeros_like(acc3_ref)
    live = flag_ref[1]

    y_ref[...] = jnp.zeros_like(y_ref)
    sn_ref[...] = srcn_ref[0 : nodes // 128, :]

    def tile(n, _):
        here = pl.ds(pl.multiple_of(n * TILE, TILE), TILE)
        w = w_ref[n]
        src = jnp.transpose(src_ref[here, :]).astype(F32)
        src_next = jnp.concatenate([sn_ref[pl.ds(2 * n, 1), :], sn_ref[pl.ds(2 * n + 1, 1), :]], axis=1)
        res, after, ru2 = residual(w, row_ref[n, 0:1, :], row_ref[n, 1:2, :], src, src_next)
        rn = live * after
        rn_ref[n] = jnp.broadcast_to(rn, (8, TILE))
        y_ref[...] += (w[rank : 2 * rank].astype(F32) + w[3 * rank : 4 * rank].astype(F32)) * rn
        r_hi, r_lo = halves(res)
        c_hi, c_lo = halves(3.0 * ru2 * res)
        acc1_ref[...] += dot(w[0 : 4 * rank], r_hi, 1, 1)
        acc2_ref[...] += dot(w[0 : 2 * rank], r_lo, 1, 1)
        s = w[4 * rank : 5 * rank]
        acc3_ref[...] += dot(
            jnp.concatenate([s, s], axis=1), jnp.concatenate([c_hi, c_lo], axis=1), 1, 1
        )
        g_ref[n, 0 : 2 * rank, :] = dot(tt_ref[...], jnp.concatenate([r_hi, r_lo], axis=0), 1, 0)
        g_ref[n, 2 * rank : 3 * rank, :] = dot(tt_ref[0:rank, :], jnp.concatenate([c_hi, c_lo], axis=0), 1, 0)
        return 0

    lax.fori_loop(0, nodes // TILE, tile, 0, unroll=UNROLL)

    n_edge = nodes // TILE
    src = jnp.transpose(edge_ref[...]).astype(F32)
    res, _, _ = residual(w_ref[n_edge], row_ref[n_edge, 0:1, :], row_ref[n_edge, 1:2, :], src, 0.0)
    r_hi, r_lo = halves(res)
    g_ref[n_edge, 0:rank, :] = dot(tt_ref[0:rank, :], jnp.concatenate([r_hi, r_lo], axis=0), 1, 0)

    y_next = jnp.sum(y_ref[...], axis=1, keepdims=True)

    for base, ref in ((0, gs_own_ref), (half, gs_oth_ref)):
        def finish(i, _, base=base, ref=ref):
            at = pl.multiple_of(i * 8, 8)
            to = pl.multiple_of(base + i * 8, 8)
            tl = tlast_ref[pl.ds(to, 8), :]

            def keep(c, value, v):
                if c in (0, n_tile - 1):
                    return
                sl = slice(c * PAD, (c + 1) * PAD)
                here = slice((c - 1) * PAD, c * PAD)
                m = band_ref[8 * (2 * W + 1) : 8 * (2 * W + 2), sl]
                k, lanes = place(c)
                g2 = g_ref[k, pl.ds(to + rank, 8), lanes]
                g3 = g_ref[k, pl.ds(to + 2 * rank, 8), lanes]
                ref[pl.ds(at, 8), here] = value - m * (g2 + tl * rn_ref[k, :, lanes]) + g3

            at_tile = [place(c) for c in range(n_tile)]
            banded([g_ref[k, pl.ds(to, 8), lanes] for k, lanes in at_tile], keep)
            return 0

        lax.fori_loop(0, half // 8, finish, 0)

    zb = acc1_ref[rank : 2 * rank, :] + acc1_ref[3 * rank : 4 * rank, :] + acc2_ref[rank : 2 * rank, :]
    za = acc1_ref[0:rank, :] + acc1_ref[2 * rank : 3 * rank, :] + acc2_ref[0:rank, :] + acc3_ref[...]
    shifted = pltpu.roll(zb, steps - 1, 1)
    gt_ref[...] = za - jnp.where(lane == steps - 1, y_next, shifted)


def body(space_factor, time_factor, initial_state, link, conductivity, mass, reaction, source):
    own_rank, nodes = space_factor.shape
    time_rank, steps = time_factor.shape
    n_space = lax.axis_size("space")
    n_tm = lax.axis_size("tm")
    n_z = n_tm // 2
    rank = own_rank * n_tm
    ext = nodes + 2 * PAD
    t_id = lax.axis_index("tm")
    x_id = t_id % 2
    z_groups = [[2 * z + x for z in range(n_z)] for x in range(2)]
    pair = [(i, i ^ 1) for i in range(n_tm)]
    as_row = lambda a: a.reshape(1, nodes)
    coefs = [as_row(conductivity), as_row(link), as_row(mass), as_row(reaction), as_row(initial_state)]

    ends = []
    specs = []
    n_end = nodes // PAD - 1
    for a in [space_factor] + coefs:
        ends += [a, a]
        specs += [
            pl.BlockSpec((a.shape[0], PAD), lambda i: (0, 0)),
            pl.BlockSpec((a.shape[0], PAD), lambda i: (0, n_end)),
        ]
    ends += [source, source, source, time_factor]
    specs += [
        pl.BlockSpec((16, steps), lambda i: (0, 0)),
        pl.BlockSpec((16, steps), lambda i: (nodes // 16 - 1, 0)),
        pl.BlockSpec((nodes, PAD), lambda i: (0, 0)),
        pl.BlockSpec((time_rank, steps), lambda i: (0, 0)),
    ]
    n_row = nodes // PAD
    to_up, to_down, to_prev, to_next = pl.pallas_call(
        pack_kernel,
        grid=(1,),
        in_specs=specs,
        out_specs=[pl.BlockSpec((n, PAD), lambda i: (0, 0)) for n in (16, 16, n_row + 8, 8)],
        out_shape=[jax.ShapeDtypeStruct((n, PAD), F32) for n in (16, 16, n_row + 8, 8)],
        name="pack_ends",
    )(*ends)
    below = lax.ppermute(to_up, "space", [(i, i + 1) for i in range(n_space - 1)])
    above = lax.ppermute(to_down, "space", [(i, i - 1) for i in range(1, n_space)])
    after = lax.ppermute(to_prev, "tm", [(i, i - 1) for i in range(1, n_tm)])
    before = lax.ppermute(to_next, "tm", [(i, i + 1) for i in range(n_tm - 1)])

    s_ext = jnp.concatenate([below[0:own_rank].astype(BF), space_factor, above[0:own_rank].astype(BF)], axis=1)
    s_own = lax.all_to_all(
        jnp.broadcast_to(s_ext[None], (n_z, own_rank, ext)), "tm", 0, 0,
        axis_index_groups=z_groups, tiled=True,
    ).reshape(rank // 2, ext)
    s_own, below, above, after, before, time_factor = lax.optimization_barrier(
        (s_own, below, above, after, before, time_factor)
    )
    s_oth = lax.ppermute(s_own, "tm", pair)

    def turn(a):
        return jnp.where(x_id == 0, a, jnp.concatenate([a[own_rank:], a[:own_rank]], axis=0))

    beside = jnp.concatenate(
        [turn(after[n_row, :time_rank]), turn(before[1, :time_rank]), jnp.zeros((PAD - 2 * time_rank,), F32)]
    ).astype(BF)
    turned = turn(time_factor)
    chunk = jnp.concatenate([turned[:, :PAD], turned[:, PAD:], beside[None], jnp.zeros((7, PAD), BF)], axis=0)

    def open_src(block):
        return jnp.concatenate([block[8:12], block[12:16]], axis=1).astype(BF)

    zero = jnp.zeros((PAD - 4, steps), BF)
    edge = jnp.concatenate([zero, open_src(below), open_src(above), zero], axis=0)
    chunk, edge = lax.optimization_barrier((chunk, edge))
    in1 = lax.all_to_all(
        jnp.broadcast_to(chunk[None], (n_space,) + chunk.shape), "space", 0, 0, tiled=True
    )

    def by_half(a):
        a = a.reshape((n_z, 2, own_rank) + a.shape[2:])
        return jnp.concatenate([a[:, 0], a[:, 1]], axis=0).reshape((rank,) + a.shape[3:])

    t_perm = jnp.concatenate([by_half(in1[:, 0:time_rank]), by_half(in1[:, time_rank : 2 * time_rank])], axis=1)
    t_next = by_half(in1[:, 2 * time_rank, 0:time_rank])
    t_prev = by_half(in1[:, 2 * time_rank, time_rank : 2 * time_rank])
    t_last = t_perm[:, -1]
    tsh = jnp.concatenate([t_prev[:, None], t_perm[:, :-1]], axis=1)
    now = jnp.concatenate([t_perm, t_next[:, None], jnp.zeros((rank, 15), BF)], axis=1).T
    ago = jnp.concatenate([tsh, t_last[:, None], jnp.zeros((rank, 15), BF)], axis=1).T
    qt = jnp.concatenate([now, -ago, now, -ago], axis=1)
    tsh0 = jnp.concatenate([jnp.zeros((rank, 1), BF), t_perm[:, :-1]], axis=1)
    tt = jnp.concatenate([t_perm, tsh0], axis=0)
    tt = jnp.concatenate([tt, tt], axis=1)
    t_last = jnp.broadcast_to(t_last.astype(F32)[:, None], (rank, 128))
    flags = jnp.stack([jnp.where(t_id == 0, 1.0, 0.0), jnp.where(t_id == n_tm - 1, 0.0, 1.0)])

    vmem = pl.BlockSpec(memory_space=pltpu.VMEM)
    gs_own, gs_oth, gt = pl.pallas_call(
        compute_kernel,
        in_specs=[pl.BlockSpec(memory_space=pltpu.SMEM)] + [vmem] * 15,
        out_shape=(
            jax.ShapeDtypeStruct((rank // 2, nodes), F32),
            jax.ShapeDtypeStruct((rank // 2, nodes), F32),
            jax.ShapeDtypeStruct((rank, steps), F32),
        ),
        scratch_shapes=[
            pltpu.VMEM((ext // TILE, 5 * rank, TILE), BF),
            pltpu.VMEM((ext // TILE, 3 * rank, TILE), F32),
            pltpu.VMEM((8, ext), F32),
            pltpu.VMEM((8 * (2 * W + 2), ext), F32),
            pltpu.VMEM((ext // TILE, 8, TILE), F32),
            pltpu.VMEM((nodes // 128, 128), F32),
            pltpu.VMEM((ext // TILE, 8, TILE), F32),
            pltpu.VMEM((rank, TILE), F32),
            pltpu.VMEM((4 * rank, steps), F32),
            pltpu.VMEM((2 * rank, steps), F32),
            pltpu.VMEM((rank, steps), F32),
        ],
        compiler_params=pltpu.CompilerParams(vmem_limit_bytes=48 * 1024 * 1024),
        name="residual_gradient",
    )(flags, s_own, s_oth, tt, qt, t_last, below, above, *coefs, after, source, edge)

    came = lax.ppermute(gs_oth, "tm", pair)
    gt = gt.reshape(2, n_space, own_rank, steps).transpose(1, 0, 2, 3).reshape(n_space, time_rank, steps)
    gt_in = lax.all_to_all(gt, "space", 0, 0, tiled=True)
    chunk_rows = own_rank * n_row + 8
    part = pl.pallas_call(
        encode_kernel,
        out_shape=jax.ShapeDtypeStruct((n_z, chunk_rows, PAD), jnp.int16),
        scratch_shapes=[pltpu.VMEM(((rank // 2) * n_row + 8 * n_z, PAD), F32)],
        name="encode_sums",
    )(gs_own, came)
    part = lax.all_to_all(part, "tm", 0, 0, axis_index_groups=z_groups, tiled=True)
    part, gt_in = lax.optimization_barrier((part, gt_in))
    grad_space = pl.pallas_call(
        functools.partial(decode_kernel, 1.0 / math.sqrt(steps * n_tm)),
        out_shape=jax.ShapeDtypeStruct((own_rank, nodes), F32),
        name="decode_sums",
    )(part)

    gt = jnp.sum(gt_in, axis=0)
    swapped = jnp.concatenate([gt[own_rank:], gt[:own_rank]], axis=0)
    grad_time = jnp.where(x_id == 0, gt, swapped) * (1.0 / math.sqrt(nodes * n_space))
    return grad_space, grad_time


def solution(mesh):
    in_specs = (
        P("tm", "space"), P("space", "tm"), P("space"), P("space"),
        P("space"), P("space"), P("space"), P("space", "tm"),
    )
    out_specs = (P("tm", "space"), P("space", "tm"))

    return jax.shard_map(body, mesh=mesh, in_specs=in_specs, out_specs=out_specs, check_vma=False)
```

time: 600 us -> 131 us (0.22)
  waiting for transfers between devices: 413 us -> 19.8 us
  blocking collectives: 91 us -> 27.8 us
  other arithmetic: 47.6 us -> 2.21 us
  starting transfers between devices: 18 us -> 51.4 us
  Pallas kernels: 0 us -> 21.5 us
  between operations: 15.6 us -> 1.02 us
    unnamed x4 -> x0, waiting for transfers between devices: 412 us -> none
    all_gather x2 -> x0, blocking collectives: 91 us -> none  [the longest x1 72.3 us: body(): space_full = lax.all_gather(space_factor, 'tm', axis=0, tiled=True)]
    all_to_all x0 -> x3, starting transfers between devices: none -> 34.5 us  [the longest x1 15.2 us: body(): lax.all_to_all(jnp.broadcast_to(s_ext[None], (n_z, own_rank, ext)), 'tm',...]
    all_to_all x0 -> x1, blocking collectives: none -> 27.8 us  [body(): lax.all_to_all(part, 'tm', 0, 0, axis_index_groups=z_groups, tiled=True)]
    sub x1 -> x0, other arithmetic: 22.1 us -> none  [body(): mass_col * (state - earlier) + diffuse(padded, rates_padded, node_count)]
    convert_element_type x1 -> x0, other arithmetic: 21.7 us -> none  [body(): descent_b = descent.astype(jnp.bfloat16)]
    pallas_call x0 -> x4, Pallas kernels: none -> 21.5 us  [the longest x1 15 us: body(): pl.pallas_call(compute_kernel, in_specs=[pl.BlockSpec(memory_space=pltpu....]
    all_to_all x0 -> x3, waiting for transfers between devices: none -> 10.5 us  [the longest x1 7.39 us: body(): lax.all_to_all(jnp.broadcast_to(s_ext[None], (n_z, own_rank, ext)), 'tm',...]
  transfers between devices with their start and end apart: 9 -> 9, of which waited for: 3 -> 6; matrix products, arithmetic and copies ran while one was open for 2% -> 3% of each run, Pallas kernels for 0% -> 2%
where the time goes in v1:
time: 131 us; the launch traced here: 129 us
  starting transfers between devices  51.4 us (39%)
  blocking collectives  27.8 us (21%)
  Pallas kernels  21.5 us (16%)
  waiting for transfers between devices  19.8 us (15%)
  local copies, waits for them, and re-layouts  5.53 us (4%)
  other arithmetic  2.21 us (2%)
    all_to_all x1, blocking collectives, body(): lax.all_to_all(part, 'tm', 0, 0, axis_index_groups=z_groups, tiled=True)  27.8 us
    all_to_all x1, starting transfers between devices, body(): lax.all_to_all(jnp.broadcast_to(s_ext[None], (n_z, own_rank, ext)), 'tm',...  15.2 us
    pallas_call x1, Pallas kernels, body(): pl.pallas_call(compute_kernel, in_specs=[pl.BlockSpec(memory_space=pltpu....  15 us
    all_to_all x1, starting transfers between devices, body(): lax.all_to_all(jnp.broadcast_to(chunk[None], (n_space,) + chunk.shape), '...  11.5 us
    all_to_all x1, starting transfers between devices, body(): gt_in = lax.all_to_all(gt, 'space', 0, 0, tiled=True)  7.81 us
    all_to_all x1, waiting for transfers between devices, body(): lax.all_to_all(jnp.broadcast_to(s_ext[None], (n_z, own_rank, ext)), 'tm',...  7.39 us
    ppermute x1, starting transfers between devices, body(): before = lax.ppermute(to_next, 'tm', [(i, i + 1) for i in range(n_tm - 1)])  4.53 us
    ppermute x1, waiting for transfers between devices, body(): came = lax.ppermute(gs_oth, 'tm', pair)  4.32 us
  transfers between devices with their start and end apart: 9, of which 6 were waited for; matrix products, arithmetic and copies ran while one was open for 3% of the time, Pallas kernels for 2%

profile of v1, /device:TPU:24, one launch (start us, length us, event | category | flops | bytes accessed | tf_op | source)
XLA Modules:
  0.0 129.2 jit_solution(9992595729205722682)
XLA Ops:
  0.6 2.4 %pack_ends.1 = (f32[16,128]{1,0:T(8,128)}, f32[16,128]{1,0:T(8,128)}, f32[40,128]{1,0:T(8,128)}, f32[8,128]{1,0:T(8,128)}) custom-call(bf16[2,4096]{1,0:T(2,128)(2,1)} %s_hi.1, bf16[2,4096]{1,0:T(2,128)(2,1)} %s_hi.1, f32[1,4096]{1,0:T(1,128)} %bitcast.47, f32[1,4096]{1,0:T(1,128)} %bitcast.48, s32[1,4096]{1,0:T(1,128)} %bitcast.50, s32[1,4096]{1,0:T(1,128)} %bitcast.51, ...), custom_call_target="tpu_custom_call" | custom-call | tf_op jit(solution)/shard_map/pack_ends/pallas_call | solution.py:304
  3.1 2.1 %collective-permute-start = (f32[16,128]{1,0:T(8,128)}, f32[16,128]{1,0:T(8,128)S(1)}, u32[]{:S(2)}, u32[]{:S(2)}) collective-permute-start(f32[16,128]{1,0:T(8,128)} %get-tuple-element.19), channel_id=1, source_target_pairs={{0,32},{32,64},{64,96},{96,128},{128,160},{160,192},{192,224},{224... | collective-permute-start | bytes 24584 | tf_op jit(solution)/shard_map/ppermute | solution.py:312
  5.2 3.6 %collective-permute-start.1 = (f32[16,128]{1,0:T(8,128)}, f32[16,128]{1,0:T(8,128)S(1)}, u32[]{:S(2)}, u32[]{:S(2)}) collective-permute-start(f32[16,128]{1,0:T(8,128)} %get-tuple-element.20), channel_id=1, source_target_pairs={{32,0},{64,32},{96,64},{128,96},{160,128},{192,160},{224,192},{256... | collective-permute-start | bytes 24584 | tf_op jit(solution)/shard_map/ppermute | solution.py:313
  8.9 1.9 %collective-permute-done.1.above_ref = f32[16,128]{1,0:T(8,128)S(1)} collective-permute-done((f32[16,128]{1,0:T(8,128)}, f32[16,128]{1,0:T(8,128)S(1)}, u32[]{:S(2)}, u32[]{:S(2)}) %collective-permute-start.1) | collective-permute-done | bytes 8224 | tf_op jit(solution)/shard_map/ppermute | solution.py:313
  10.8 0.9 broadcast_in_dim.34
  11.6 15.2 %all-to-all-start = ((bf16[16,2,4352]{2,1,0:T(2,128)(2,1)}), bf16[16,2,4352]{2,1,0:T(2,128)(2,1)S(1)}, u32[]{:S(2)}, u32[]{:S(2)}) async-start(bf16[16,2,4352]{2,1,0:T(2,128)(2,1)} %broadcast_in_dim.34), calls=%async_computation | async-start | bytes 557056 | tf_op jit(solution)/shard_map/all_to_all | solution.py:318
  26.8 1.3 collective-permute-start.2
  28.1 0.7 convert.39
  28.8 4.5 %collective-permute-start.3 = (bf16[8,128]{1,0:T(8,128)(2,1)S(1)}, bf16[8,128]{1,0:T(8,128)(2,1)S(1)}, u32[]{:S(2)}, u32[]{:S(2)}) collective-permute-start(bf16[8,128]{1,0:T(8,128)(2,1)S(1)} %convert.39), channel_id=1, source_target_pairs={{0,1},{1,2},{2,3},{3,4},{4,5},{5,6},{6,7},{7,8},{8,9},{9,10},{10,1... | collective-permute-start | bytes 6152 | tf_op jit(solution)/shard_map/ppermute | solution.py:315
  33.6 7.4 %all-to-all-done = bf16[16,2,4352]{2,1,0:T(2,128)(2,1)S(1)} async-done(((bf16[16,2,4352]{2,1,0:T(2,128)(2,1)}), bf16[16,2,4352]{2,1,0:T(2,128)(2,1)S(1)}, u32[]{:S(2)}, u32[]{:S(2)}) %all-to-all-start) | async-done | bytes 278560 | tf_op jit(solution)/shard_map/all_to_all | solution.py:318
  42.2 11.5 %all-to-all-start.1 = ((bf16[16,16,128]{2,1,0:T(8,128)(2,1)}), bf16[16,16,128]{2,1,0:T(8,128)(2,1)S(1)}, u32[]{:S(2)}, u32[]{:S(2)}) async-start(bf16[16,16,128]{2,1,0:T(8,128)(2,1)} %broadcast_in_dim.38), calls=%async_computation.1 | async-start | bytes 131072 | tf_op jit(solution)/shard_map/all_to_all | solution.py:342
  53.8 2.7 %collective-permute-start.4 = (bf16[32,4352]{1,0:T(8,128)(2,1)S(1)}, bf16[32,4352]{1,0:T(8,128)(2,1)S(1)}, u32[]{:S(2)}, u32[]{:S(2)}) collective-permute-start(bf16[32,4352]{1,0:T(8,128)(2,1)S(1)} %reshape.89.sown_ref), channel_id=1, source_target_pairs={{0,1},{1,0},{2,3},{3,2},{4,5},{5,4},{6,7},{7,6},{8,9},{9,8},{10,11... | collective-permute-start | bytes 835592 | tf_op jit(solution)/shard_map/ppermute | solution.py:325
  56.4 3.0 %all-to-all-done.1 = bf16[16,16,128]{2,1,0:T(8,128)(2,1)S(1)} async-done(((bf16[16,16,128]{2,1,0:T(8,128)(2,1)}), bf16[16,16,128]{2,1,0:T(8,128)(2,1)S(1)}, u32[]{:S(2)}, u32[]{:S(2)}) %all-to-all-start.1) | async-done | bytes 65568 | tf_op jit(solution)/shard_map/all_to_all | solution.py:342
  61.3 3.0 %collective-permute-done.4.soth_ref = bf16[32,4352]{1,0:T(8,128)(2,1)S(1)} collective-permute-done((bf16[32,4352]{1,0:T(8,128)(2,1)S(1)}, bf16[32,4352]{1,0:T(8,128)(2,1)S(1)}, u32[]{:S(2)}, u32[]{:S(2)}) %collective-permute-start.4) | collective-permute-done | bytes 278560 | tf_op jit(solution)/shard_map/ppermute | solution.py:325
  64.4 15.0 %residual_gradient.1 = (f32[32,4096]{1,0:T(8,128)S(1)}, f32[32,4096]{1,0:T(8,128)}, f32[64,256]{1,0:T(8,128)S(1)}) custom-call(f32[2]{0:T(128)S(1)} %pad_maximum_fusion.6.flag_ref, bf16[32,4352]{1,0:T(8,128)(2,1)S(1)} %reshape.89.sown_ref, bf16[32,4352]{1,0:T(8,128)(2,1)S(1)} %collective-permute-done.4.soth_ref, bf16[128,512]{1,0:T(8,128)(2,1)S(1)} %copy.43.tt_ref, ...), custom_call_target="tpu_custom_call" | custom-call | tf_op jit(solution)/shard_map/residual_gradient/pallas_call | solution.py:365
  79.4 0.8 copy-done.1
  80.2 2.7 %collective-permute-start.5 = (f32[32,4096]{1,0:T(8,128)}, f32[32,4096]{1,0:T(8,128)S(1)}, u32[]{:S(2)}, u32[]{:S(2)}) collective-permute-start(f32[32,4096]{1,0:T(8,128)} %get-tuple-element.32), channel_id=1, source_target_pairs={{0,1},{1,0},{2,3},{3,2},{4,5},{5,4},{6,7},{7,6},{8,9},{9,8},{10,11... | collective-permute-start | bytes 1572872 | tf_op jit(solution)/shard_map/ppermute | solution.py:390
  82.9 0.7 copy.45
  83.6 7.8 %all-to-all-start.3 = ((f32[16,4,256]{2,1,0:T(4,128)}), f32[16,4,256]{2,1,0:T(4,128)S(1)}, u32[]{:S(2)}, u32[]{:S(2)}) async-start(f32[16,4,256]{2,1,0:T(4,128)} %copy.45), calls=%async_computation.3 | async-start | bytes 131072 | tf_op jit(solution)/shard_map/all_to_all | solution.py:392
  91.4 4.3 %collective-permute-done.5.came_ref = f32[32,4096]{1,0:T(8,128)S(1)} collective-permute-done((f32[32,4096]{1,0:T(8,128)}, f32[32,4096]{1,0:T(8,128)S(1)}, u32[]{:S(2)}, u32[]{:S(2)}) %collective-permute-start.5) | collective-permute-done | bytes 524320 | tf_op jit(solution)/shard_map/ppermute | solution.py:390
  95.7 0.8 copy-done.7
  96.6 2.5 %encode_sums.1 = s16[16,72,128]{2,1,0:T(8,128)(2,1)} custom-call(f32[32,4096]{1,0:T(8,128)} %copy-done.1, f32[32,4096]{1,0:T(8,128)} %copy-done.7), custom_call_target="tpu_custom_call" | custom-call | tf_op jit(solution)/shard_map/encode_sums/pallas_call | solution.py:394
  99.1 27.8 %all_to_all.20.in_ref = s16[16,72,128]{2,1,0:T(8,128)(2,1)} all-to-all(s16[16,72,128]{2,1,0:T(8,128)(2,1)} %encode_sums.1), channel_id=1, replica_groups={{0,2,4,6,8,10,12,14,16,18,20,22,24,26,28,30},{1,3,5,7,9,11,13,15,17,19,..., dimensions={0} | all-to-all | bytes 589824 | tf_op jit(solution)/shard_map/all_to_all | solution.py:400
  126.9 1.7 %decode_sums.1 = f32[2,4096]{1,0:T(2,128)} custom-call(s16[16,72,128]{2,1,0:T(8,128)(2,1)} %all_to_all.20.in_ref), custom_call_target="tpu_custom_call" | custom-call | tf_op jit(solution)/shard_map/decode_sums/pallas_call | solution.py:402
  (76 shorter events, 4.0 us)
Async XLA Ops:
  0.6 10.1 %copy-start.8 = (bf16[2,4096]{1,0:T(2,128)(2,1)S(1)}, bf16[2,4096]{1,0:T(2,128)(2,1)}, u32[]{:S(2)}) copy-start(bf16[2,4096]{1,0:T(2,128)(2,1)} %s_hi.1) | copy-start | bytes 49156
  0.6 40.6 %copy-start.9 = (bf16[4,256]{1,0:T(4,128)(2,1)S(1)}, bf16[4,256]{1,0:T(4,128)(2,1)}, u32[]{:S(2)}) copy-start(bf16[4,256]{1,0:T(4,128)(2,1)} %time_ref.1) | copy-start | bytes 6148
  3.1 61.3 %copy-start = (bf16[4096,256]{1,0:T(8,128)(2,1)S(1)}, bf16[4096,256]{1,0:T(8,128)(2,1)}, u32[]{:S(2)}) copy-start(bf16[4096,256]{1,0:T(8,128)(2,1)} %src_ref.1) | copy-start | bytes 6291460
  3.1 61.3 %copy-start.2 = (f32[4096]{0:T(1024)S(1)}, f32[4096]{0:T(1024)}, u32[]{:S(2)}) copy-start(f32[4096]{0:T(1024)} %param.12) | copy-start | bytes 49156
  3.1 61.3 %copy-start.3 = (s32[4096]{0:T(1024)S(1)}, s32[4096]{0:T(1024)}, u32[]{:S(2)}) copy-start(s32[4096]{0:T(1024)} %param.11) | copy-start | bytes 49156
  3.1 61.3 %copy-start.4 = (f32[4096]{0:T(1024)S(1)}, f32[4096]{0:T(1024)}, u32[]{:S(2)}) copy-start(f32[4096]{0:T(1024)} %param.13) | copy-start | bytes 49156
  3.1 61.3 %copy-start.5 = (f32[4096]{0:T(1024)S(1)}, f32[4096]{0:T(1024)}, u32[]{:S(2)}) copy-start(f32[4096]{0:T(1024)} %param.14) | copy-start | bytes 49156
  3.1 61.3 %copy-start.6 = (f32[4096]{0:T(1024)S(1)}, f32[4096]{0:T(1024)}, u32[]{:S(2)}) copy-start(f32[4096]{0:T(1024)} %param.10) | copy-start | bytes 49156
  3.1 5.7 %collective-permute-start = (f32[16,128]{1,0:T(8,128)}, f32[16,128]{1,0:T(8,128)S(1)}, u32[]{:S(2)}, u32[]{:S(2)}) collective-permute-start(f32[16,128]{1,0:T(8,128)} %get-tuple-element.19), channel_id=1, source_target_pairs={{0,32},{32,64},{64,96},{96,128},{128,160},{160,192},{192,224},{224... | collective-permute-start | bytes 24584 | tf_op jit(solution)/shard_map/ppermute | solution.py:312
  5.2 5.6 %collective-permute-start.1 = (f32[16,128]{1,0:T(8,128)}, f32[16,128]{1,0:T(8,128)S(1)}, u32[]{:S(2)}, u32[]{:S(2)}) collective-permute-start(f32[16,128]{1,0:T(8,128)} %get-tuple-element.20), channel_id=1, source_target_pairs={{32,0},{64,32},{96,64},{128,96},{160,128},{192,160},{224,192},{256... | collective-permute-start | bytes 24584 | tf_op jit(solution)/shard_map/ppermute | solution.py:313
  11.6 29.3 %all-to-all-start = ((bf16[16,2,4352]{2,1,0:T(2,128)(2,1)}), bf16[16,2,4352]{2,1,0:T(2,128)(2,1)S(1)}, u32[]{:S(2)}, u32[]{:S(2)}) async-start(bf16[16,2,4352]{2,1,0:T(2,128)(2,1)} %broadcast_in_dim.34), calls=%async_computation | async-start | bytes 557056 | tf_op jit(solution)/shard_map/all_to_all | solution.py:318
  26.8 14.2 %collective-permute-start.2 = (f32[40,128]{1,0:T(8,128)}, f32[40,128]{1,0:T(8,128)S(1)}, u32[]{:S(2)}, u32[]{:S(2)}) collective-permute-start(f32[40,128]{1,0:T(8,128)} %get-tuple-element.21), channel_id=1, source_target_pairs={{1,0},{2,1},{3,2},{4,3},{5,4},{6,5},{7,6},{8,7},{9,8},{10,9},{11,1... | collective-permute-start | bytes 61448 | tf_op jit(solution)/shard_map/ppermute | solution.py:314
  28.8 12.2 %collective-permute-start.3 = (bf16[8,128]{1,0:T(8,128)(2,1)S(1)}, bf16[8,128]{1,0:T(8,128)(2,1)S(1)}, u32[]{:S(2)}, u32[]{:S(2)}) collective-permute-start(bf16[8,128]{1,0:T(8,128)(2,1)S(1)} %convert.39), channel_id=1, source_target_pairs={{0,1},{1,2},{2,3},{3,4},{4,5},{5,6},{6,7},{7,8},{8,9},{9,10},{10,1... | collective-permute-start | bytes 6152 | tf_op jit(solution)/shard_map/ppermute | solution.py:315
  42.2 17.3 %all-to-all-start.1 = ((bf16[16,16,128]{2,1,0:T(8,128)(2,1)}), bf16[16,16,128]{2,1,0:T(8,128)(2,1)S(1)}, u32[]{:S(2)}, u32[]{:S(2)}) async-start(bf16[16,16,128]{2,1,0:T(8,128)(2,1)} %broadcast_in_dim.38), calls=%async_computation.1 | async-start | bytes 131072 | tf_op jit(solution)/shard_map/all_to_all | solution.py:342
  53.8 10.6 %collective-permute-start.4 = (bf16[32,4352]{1,0:T(8,128)(2,1)S(1)}, bf16[32,4352]{1,0:T(8,128)(2,1)S(1)}, u32[]{:S(2)}, u32[]{:S(2)}) collective-permute-start(bf16[32,4352]{1,0:T(8,128)(2,1)S(1)} %reshape.89.sown_ref), channel_id=1, source_target_pairs={{0,1},{1,0},{2,3},{3,2},{4,5},{5,4},{6,7},{7,6},{8,9},{9,8},{10,11... | collective-permute-start | bytes 835592 | tf_op jit(solution)/shard_map/ppermute | solution.py:325
  79.4 0.8 copy-start.1
  80.2 15.5 %collective-permute-start.5 = (f32[32,4096]{1,0:T(8,128)}, f32[32,4096]{1,0:T(8,128)S(1)}, u32[]{:S(2)}, u32[]{:S(2)}) collective-permute-start(f32[32,4096]{1,0:T(8,128)} %get-tuple-element.32), channel_id=1, source_target_pairs={{0,1},{1,0},{2,3},{3,2},{4,5},{5,4},{6,7},{7,6},{8,9},{9,8},{10,11... | collective-permute-start | bytes 1572872 | tf_op jit(solution)/shard_map/ppermute | solution.py:390
  83.6 15.5 %all-to-all-start.3 = ((f32[16,4,256]{2,1,0:T(4,128)}), f32[16,4,256]{2,1,0:T(4,128)S(1)}, u32[]{:S(2)}, u32[]{:S(2)}) async-start(f32[16,4,256]{2,1,0:T(4,128)} %copy.45), calls=%async_computation.3 | async-start | bytes 131072 | tf_op jit(solution)/shard_map/all_to_all | solution.py:392
  95.7 0.8 copy-start.7

commit v2 on v1

--- a/solution.py
+++ b/solution.py
@@ -12,7 +12,7 @@
 W = 4
 PAD = 128
 TILE = 256
-UNROLL = 2
+UNROLL = 4
 BF = jnp.bfloat16
 F32 = jnp.float32
 
@@ -53,6 +53,11 @@
     next_ref[...] = ends
 
 
+def power_of(v):
+    top = jnp.max(jnp.abs(v), axis=1, keepdims=True)
+    return jnp.ceil(jnp.log2(jnp.maximum(top, 1e-30)) + 0.01) - 15.0
+
+
 def encode_kernel(own_ref, came_ref, out_ref, flat_ref):
     rows, nodes = own_ref.shape
     n_row = nodes // PAD
@@ -60,9 +65,10 @@
     own_rank = rows // n_z
     body = own_rank * n_row
     for g in range(rows // 8):
-        v = own_ref[8 * g : 8 * g + 8, :] + came_ref[8 * g : 8 * g + 8, :]
-        top = jnp.max(jnp.abs(v), axis=1, keepdims=True)
-        power = jnp.ceil(jnp.log2(jnp.maximum(top, 1e-30)) + 0.01) - 15.0
+        step = jnp.exp2(came_ref[8 * g : 8 * g + 8, nodes:].astype(jnp.int32).astype(F32))[:, 0:1]
+        v = own_ref[8 * g : 8 * g + 8, :]
+        v = v + came_ref[8 * g : 8 * g + 8, 0:nodes].astype(jnp.int32).astype(F32) * step
+        power = power_of(v)
         q = jnp.floor(v * jnp.exp2(-power) + 0.5)
         for c in range(n_row):
             flat_ref[pl.ds(8 * g * n_row + c, 8, stride=n_row), :] = q[:, c * PAD : (c + 1) * PAD]
@@ -100,7 +106,7 @@
     flag_ref, sown_ref, soth_ref, tt_ref, qt_ref, tlast_ref,
     below_ref, above_ref, cond_ref, link_ref, mass_ref, reac_ref, init_ref, srcn_ref, src_ref, edge_ref,
     gs_own_ref, gs_oth_ref, gt_ref,
-    w_ref, g_ref, coef_ref, band_ref, row_ref, sn_ref, rn_ref, y_ref, acc1_ref, acc2_ref, acc3_ref,
+    w_ref, g_ref, coef_ref, band_ref, row_ref, sn_ref, rn_ref, y_ref, st_ref, acc1_ref, acc2_ref, acc3_ref,
 ):
     ext = coef_ref.shape[1]
     nodes = ext - 2 * PAD
@@ -255,10 +261,20 @@
                 k, lanes = place(c)
                 g2 = g_ref[k, pl.ds(to + rank, 8), lanes]
                 g3 = g_ref[k, pl.ds(to + 2 * rank, 8), lanes]
-                ref[pl.ds(at, 8), here] = value - m * (g2 + tl * rn_ref[k, :, lanes]) + g3
+                value = value - m * (g2 + tl * rn_ref[k, :, lanes]) + g3
+                if base:
+                    st_ref[:, here] = value
+                else:
+                    ref[pl.ds(at, 8), here] = value
 
             at_tile = [place(c) for c in range(n_tile)]
             banded([g_ref[k, pl.ds(to, 8), lanes] for k, lanes in at_tile], keep)
+            if base:
+                v = st_ref[...]
+                power = power_of(v)
+                q = jnp.floor(v * jnp.exp2(-power) + 0.5)
+                ref[pl.ds(at, 8), 0:nodes] = q.astype(jnp.int32).astype(jnp.int16)
+                ref[pl.ds(at, 8), nodes:] = jnp.broadcast_to(power, (8, PAD)).astype(jnp.int32).astype(jnp.int16)
             return 0
 
         lax.fori_loop(0, half // 8, finish, 0)
@@ -367,7 +383,7 @@
         in_specs=[pl.BlockSpec(memory_space=pltpu.SMEM)] + [vmem] * 15,
         out_shape=(
             jax.ShapeDtypeStruct((rank // 2, nodes), F32),
-            jax.ShapeDtypeStruct((rank // 2, nodes), F32),
+            jax.ShapeDtypeStruct((rank // 2, nodes + PAD), jnp.int16),
             jax.ShapeDtypeStruct((rank, steps), F32),
         ),
         scratch_shapes=[
@@ -379,6 +395,7 @@
             pltpu.VMEM((nodes // 128, 128), F32),
             pltpu.VMEM((ext // TILE, 8, TILE), F32),
             pltpu.VMEM((rank, TILE), F32),
+            pltpu.VMEM((8, nodes), F32),
             pltpu.VMEM((4 * rank, steps), F32),
             pltpu.VMEM((2 * rank, steps), F32),
             pltpu.VMEM((rank, steps), F32),

time: 131 us -> 128 us (0.977)
  waiting for transfers between devices: 19.8 us -> 18 us
    ppermute x1, waiting for transfers between devices: 4.32 us -> 0.01 us  [body(): came = lax.ppermute(gs_oth, 'tm', pair)]
    all_to_all x1, waiting for transfers between devices: 0.1 us -> 2.61 us  [body(): gt_in = lax.all_to_all(gt, 'space', 0, 0, tiled=True)]
  transfers between devices with their start and end apart: 9 -> 9, of which waited for: 6 -> 5; matrix products, arithmetic and copies ran while one was open for 3% -> 3% of each run, Pallas kernels for 2% -> 2%
where the time goes in v2:
time: 128 us; the launch traced here: 126 us
  starting transfers between devices  51.4 us (40%)
  blocking collectives  27.8 us (22%)
  Pallas kernels  20.6 us (16%)
  waiting for transfers between devices  18 us (14%)
  local copies, waits for them, and re-layouts  5.4 us (4%)
  other arithmetic  2.21 us (2%)
    all_to_all x1, blocking collectives, body(): lax.all_to_all(part, 'tm', 0, 0, axis_index_groups=z_groups, tiled=True)  27.8 us
    all_to_all x1, starting transfers between devices, body(): lax.all_to_all(jnp.broadcast_to(s_ext[None], (n_z, own_rank, ext)), 'tm',...  15.2 us
    pallas_call x1, Pallas kernels, body(): pl.pallas_call(compute_kernel, in_specs=[pl.BlockSpec(memory_space=pltpu....  14 us
    all_to_all x1, starting transfers between devices, body(): lax.all_to_all(jnp.broadcast_to(chunk[None], (n_space,) + chunk.shape), '...  11.5 us
    all_to_all x1, starting transfers between devices, body(): gt_in = lax.all_to_all(gt, 'space', 0, 0, tiled=True)  7.83 us
    all_to_all x1, waiting for transfers between devices, body(): lax.all_to_all(jnp.broadcast_to(s_ext[None], (n_z, own_rank, ext)), 'tm',...  7.39 us
    ppermute x1, starting transfers between devices, body(): before = lax.ppermute(to_next, 'tm', [(i, i + 1) for i in range(n_tm - 1)])  4.53 us
    ppermute x1, starting transfers between devices, body(): lax.ppermute(to_down, 'space', [(i, i - 1) for i in range(1, n_space)])  3.64 us
  transfers between devices with their start and end apart: 9, of which 5 were waited for; matrix products, arithmetic and copies ran while one was open for 3% of the time, Pallas kernels for 2%

profile of v2, /device:TPU:24, one launch (start us, length us, event | category | flops | bytes accessed | tf_op | source)
XLA Modules:
  0.0 126.4 jit_solution(13831228827501809254)
XLA Ops:
  0.6 2.4 %pack_ends.1 = (f32[16,128]{1,0:T(8,128)}, f32[16,128]{1,0:T(8,128)}, f32[40,128]{1,0:T(8,128)}, f32[8,128]{1,0:T(8,128)}) custom-call(bf16[2,4096]{1,0:T(2,128)(2,1)} %s_hi.1, bf16[2,4096]{1,0:T(2,128)(2,1)} %s_hi.1, f32[1,4096]{1,0:T(1,128)} %bitcast.47, f32[1,4096]{1,0:T(1,128)} %bitcast.48, s32[1,4096]{1,0:T(1,128)} %bitcast.50, s32[1,4096]{1,0:T(1,128)} %bitcast.51, ...), custom_call_target="tpu_custom_call" | custom-call | tf_op jit(solution)/shard_map/pack_ends/pallas_call | solution.py:320
  3.1 2.1 %collective-permute-start = (f32[16,128]{1,0:T(8,128)}, f32[16,128]{1,0:T(8,128)S(1)}, u32[]{:S(2)}, u32[]{:S(2)}) collective-permute-start(f32[16,128]{1,0:T(8,128)} %get-tuple-element.19), channel_id=1, source_target_pairs={{0,32},{32,64},{64,96},{96,128},{128,160},{160,192},{192,224},{224... | collective-permute-start | bytes 24584 | tf_op jit(solution)/shard_map/ppermute | solution.py:328
  5.2 3.6 %collective-permute-start.1 = (f32[16,128]{1,0:T(8,128)}, f32[16,128]{1,0:T(8,128)S(1)}, u32[]{:S(2)}, u32[]{:S(2)}) collective-permute-start(f32[16,128]{1,0:T(8,128)} %get-tuple-element.20), channel_id=1, source_target_pairs={{32,0},{64,32},{96,64},{128,96},{160,128},{192,160},{224,192},{256... | collective-permute-start | bytes 24584 | tf_op jit(solution)/shard_map/ppermute | solution.py:329
  8.9 1.9 %collective-permute-done.1.above_ref = f32[16,128]{1,0:T(8,128)S(1)} collective-permute-done((f32[16,128]{1,0:T(8,128)}, f32[16,128]{1,0:T(8,128)S(1)}, u32[]{:S(2)}, u32[]{:S(2)}) %collective-permute-start.1) | collective-permute-done | bytes 8224 | tf_op jit(solution)/shard_map/ppermute | solution.py:329
  10.8 0.9 broadcast_in_dim.34
  11.6 15.2 %all-to-all-start = ((bf16[16,2,4352]{2,1,0:T(2,128)(2,1)}), bf16[16,2,4352]{2,1,0:T(2,128)(2,1)S(1)}, u32[]{:S(2)}, u32[]{:S(2)}) async-start(bf16[16,2,4352]{2,1,0:T(2,128)(2,1)} %broadcast_in_dim.34), calls=%async_computation | async-start | bytes 557056 | tf_op jit(solution)/shard_map/all_to_all | solution.py:334
  26.8 1.3 %collective-permute-start.2 = (f32[40,128]{1,0:T(8,128)}, f32[40,128]{1,0:T(8,128)S(1)}, u32[]{:S(2)}, u32[]{:S(2)}) collective-permute-start(f32[40,128]{1,0:T(8,128)} %get-tuple-element.21), channel_id=1, source_target_pairs={{1,0},{2,1},{3,2},{4,3},{5,4},{6,5},{7,6},{8,7},{9,8},{10,9},{11,1... | collective-permute-start | bytes 61448 | tf_op jit(solution)/shard_map/ppermute | solution.py:330
  28.1 0.7 convert.39
  28.8 4.5 %collective-permute-start.3 = (bf16[8,128]{1,0:T(8,128)(2,1)S(1)}, bf16[8,128]{1,0:T(8,128)(2,1)S(1)}, u32[]{:S(2)}, u32[]{:S(2)}) collective-permute-start(bf16[8,128]{1,0:T(8,128)(2,1)S(1)} %convert.39), channel_id=1, source_target_pairs={{0,1},{1,2},{2,3},{3,4},{4,5},{5,6},{6,7},{7,8},{8,9},{9,10},{10,1... | collective-permute-start | bytes 6152 | tf_op jit(solution)/shard_map/ppermute | solution.py:331
  33.6 7.4 %all-to-all-done = bf16[16,2,4352]{2,1,0:T(2,128)(2,1)S(1)} async-done(((bf16[16,2,4352]{2,1,0:T(2,128)(2,1)}), bf16[16,2,4352]{2,1,0:T(2,128)(2,1)S(1)}, u32[]{:S(2)}, u32[]{:S(2)}) %all-to-all-start) | async-done | bytes 278560 | tf_op jit(solution)/shard_map/all_to_all | solution.py:334
  42.1 11.5 %all-to-all-start.1 = ((bf16[16,16,128]{2,1,0:T(8,128)(2,1)}), bf16[16,16,128]{2,1,0:T(8,128)(2,1)S(1)}, u32[]{:S(2)}, u32[]{:S(2)}) async-start(bf16[16,16,128]{2,1,0:T(8,128)(2,1)} %broadcast_in_dim.38), calls=%async_computation.1 | async-start | bytes 131072 | tf_op jit(solution)/shard_map/all_to_all | solution.py:358
  53.8 2.7 %collective-permute-start.4 = (bf16[32,4352]{1,0:T(8,128)(2,1)S(1)}, bf16[32,4352]{1,0:T(8,128)(2,1)S(1)}, u32[]{:S(2)}, u32[]{:S(2)}) collective-permute-start(bf16[32,4352]{1,0:T(8,128)(2,1)S(1)} %reshape.89.sown_ref), channel_id=1, source_target_pairs={{0,1},{1,0},{2,3},{3,2},{4,5},{5,4},{6,7},{7,6},{8,9},{9,8},{10,11... | collective-permute-start | bytes 835592 | tf_op jit(solution)/shard_map/ppermute | solution.py:341
  56.4 3.0 %all-to-all-done.1 = bf16[16,16,128]{2,1,0:T(8,128)(2,1)S(1)} async-done(((bf16[16,16,128]{2,1,0:T(8,128)(2,1)}), bf16[16,16,128]{2,1,0:T(8,128)(2,1)S(1)}, u32[]{:S(2)}, u32[]{:S(2)}) %all-to-all-start.1) | async-done | bytes 65568 | tf_op jit(solution)/shard_map/all_to_all | solution.py:358
  61.3 3.0 %collective-permute-done.4.soth_ref = bf16[32,4352]{1,0:T(8,128)(2,1)S(1)} collective-permute-done((bf16[32,4352]{1,0:T(8,128)(2,1)S(1)}, bf16[32,4352]{1,0:T(8,128)(2,1)S(1)}, u32[]{:S(2)}, u32[]{:S(2)}) %collective-permute-start.4) | collective-permute-done | bytes 278560 | tf_op jit(solution)/shard_map/ppermute | solution.py:341
  64.4 14.0 %residual_gradient.1 = (f32[32,4096]{1,0:T(8,128)S(1)}, s16[32,4224]{1,0:T(8,128)(2,1)S(1)}, f32[64,256]{1,0:T(8,128)S(1)}) custom-call(f32[2]{0:T(128)S(1)} %pad_maximum_fusion.6.flag_ref, bf16[32,4352]{1,0:T(8,128)(2,1)S(1)} %reshape.89.sown_ref, bf16[32,4352]{1,0:T(8,128)(2,1)S(1)} %collective-permute-done.4.soth_ref, bf16[128,512]{1,0:T(8,128)(2,1)S(1)} %copy.43.tt_ref, ...), custom_call_target="tpu_custom_call" | custom-call | tf_op jit(solution)/shard_map/residual_gradient/pallas_call | solution.py:381
  78.5 0.8 copy-done.1
  79.3 2.7 %collective-permute-start.5 = (s16[32,4224]{1,0:T(8,128)(2,1)S(1)}, s16[32,4224]{1,0:T(8,128)(2,1)S(1)}, u32[]{:S(2)}, u32[]{:S(2)}) collective-permute-start(s16[32,4224]{1,0:T(8,128)(2,1)S(1)} %get-tuple-element.32), channel_id=1, source_target_pairs={{0,1},{1,0},{2,3},{3,2},{4,5},{5,4},{6,7},{7,6},{8,9},{9,8},{10,11... | collective-permute-start | bytes 811016 | tf_op jit(solution)/shard_map/ppermute | solution.py:407
  82.0 0.7 copy.45
  82.7 7.8 %all-to-all-start.3 = ((f32[16,4,256]{2,1,0:T(4,128)}), f32[16,4,256]{2,1,0:T(4,128)S(1)}, u32[]{:S(2)}, u32[]{:S(2)}) async-start(f32[16,4,256]{2,1,0:T(4,128)} %copy.45), calls=%async_computation.3 | async-start | bytes 131072 | tf_op jit(solution)/shard_map/all_to_all | solution.py:409
  90.5 0.7 copy-done.7
  91.2 2.5 %encode_sums.1 = s16[16,72,128]{2,1,0:T(8,128)(2,1)} custom-call(f32[32,4096]{1,0:T(8,128)} %copy-done.1, s16[32,4224]{1,0:T(8,128)(2,1)} %copy-done.7), custom_call_target="tpu_custom_call" | custom-call | tf_op jit(solution)/shard_map/encode_sums/pallas_call | solution.py:411
  93.7 2.6 %all-to-all-done.3 = f32[16,4,256]{2,1,0:T(4,128)S(1)} async-done(((f32[16,4,256]{2,1,0:T(4,128)}), f32[16,4,256]{2,1,0:T(4,128)S(1)}, u32[]{:S(2)}, u32[]{:S(2)}) %all-to-all-start.3) | async-done | bytes 65568 | tf_op jit(solution)/shard_map/all_to_all | solution.py:409
  96.3 27.8 %all_to_all.20.in_ref = s16[16,72,128]{2,1,0:T(8,128)(2,1)} all-to-all(s16[16,72,128]{2,1,0:T(8,128)(2,1)} %encode_sums.1), channel_id=1, replica_groups={{0,2,4,6,8,10,12,14,16,18,20,22,24,26,28,30},{1,3,5,7,9,11,13,15,17,19,..., dimensions={0} | all-to-all | bytes 589824 | tf_op jit(solution)/shard_map/all_to_all | solution.py:417
  124.1 1.7 %decode_sums.1 = f32[2,4096]{1,0:T(2,128)} custom-call(s16[16,72,128]{2,1,0:T(8,128)(2,1)} %all_to_all.20.in_ref), custom_call_target="tpu_custom_call" | custom-call | tf_op jit(solution)/shard_map/decode_sums/pallas_call | solution.py:419
  (76 shorter events, 3.9 us)
Async XLA Ops:
  0.6 10.1 %copy-start.8 = (bf16[2,4096]{1,0:T(2,128)(2,1)S(1)}, bf16[2,4096]{1,0:T(2,128)(2,1)}, u32[]{:S(2)}) copy-start(bf16[2,4096]{1,0:T(2,128)(2,1)} %s_hi.1) | copy-start | bytes 49156
  0.6 40.6 %copy-start.9 = (bf16[4,256]{1,0:T(4,128)(2,1)S(1)}, bf16[4,256]{1,0:T(4,128)(2,1)}, u32[]{:S(2)}) copy-start(bf16[4,256]{1,0:T(4,128)(2,1)} %time_ref.1) | copy-start | bytes 6148
  3.1 61.3 %copy-start = (bf16[4096,256]{1,0:T(8,128)(2,1)S(1)}, bf16[4096,256]{1,0:T(8,128)(2,1)}, u32[]{:S(2)}) copy-start(bf16[4096,256]{1,0:T(8,128)(2,1)} %src_ref.1) | copy-start | bytes 6291460
  3.1 61.3 %copy-start.2 = (f32[4096]{0:T(1024)S(1)}, f32[4096]{0:T(1024)}, u32[]{:S(2)}) copy-start(f32[4096]{0:T(1024)} %param.12) | copy-start | bytes 49156
  3.1 61.3 %copy-start.3 = (s32[4096]{0:T(1024)S(1)}, s32[4096]{0:T(1024)}, u32[]{:S(2)}) copy-start(s32[4096]{0:T(1024)} %param.11) | copy-start | bytes 49156
  3.1 61.3 %copy-start.4 = (f32[4096]{0:T(1024)S(1)}, f32[4096]{0:T(1024)}, u32[]{:S(2)}) copy-start(f32[4096]{0:T(1024)} %param.13) | copy-start | bytes 49156
  3.1 61.3 %copy-start.5 = (f32[4096]{0:T(1024)S(1)}, f32[4096]{0:T(1024)}, u32[]{:S(2)}) copy-start(f32[4096]{0:T(1024)} %param.14) | copy-start | bytes 49156
  3.1 61.3 %copy-start.6 = (f32[4096]{0:T(1024)S(1)}, f32[4096]{0:T(1024)}, u32[]{:S(2)}) copy-start(f32[4096]{0:T(1024)} %param.10) | copy-start | bytes 49156
  3.1 5.7 %collective-permute-start = (f32[16,128]{1,0:T(8,128)}, f32[16,128]{1,0:T(8,128)S(1)}, u32[]{:S(2)}, u32[]{:S(2)}) collective-permute-start(f32[16,128]{1,0:T(8,128)} %get-tuple-element.19), channel_id=1, source_target_pairs={{0,32},{32,64},{64,96},{96,128},{128,160},{160,192},{192,224},{224... | collective-permute-start | bytes 24584 | tf_op jit(solution)/shard_map/ppermute | solution.py:328
  5.2 5.6 %collective-permute-start.1 = (f32[16,128]{1,0:T(8,128)}, f32[16,128]{1,0:T(8,128)S(1)}, u32[]{:S(2)}, u32[]{:S(2)}) collective-permute-start(f32[16,128]{1,0:T(8,128)} %get-tuple-element.20), channel_id=1, source_target_pairs={{32,0},{64,32},{96,64},{128,96},{160,128},{192,160},{224,192},{256... | collective-permute-start | bytes 24584 | tf_op jit(solution)/shard_map/ppermute | solution.py:329
  11.6 29.3 %all-to-all-start = ((bf16[16,2,4352]{2,1,0:T(2,128)(2,1)}), bf16[16,2,4352]{2,1,0:T(2,128)(2,1)S(1)}, u32[]{:S(2)}, u32[]{:S(2)}) async-start(bf16[16,2,4352]{2,1,0:T(2,128)(2,1)} %broadcast_in_dim.34), calls=%async_computation | async-start | bytes 557056 | tf_op jit(solution)/shard_map/all_to_all | solution.py:334
  26.8 14.2 %collective-permute-start.2 = (f32[40,128]{1,0:T(8,128)}, f32[40,128]{1,0:T(8,128)S(1)}, u32[]{:S(2)}, u32[]{:S(2)}) collective-permute-start(f32[40,128]{1,0:T(8,128)} %get-tuple-element.21), channel_id=1, source_target_pairs={{1,0},{2,1},{3,2},{4,3},{5,4},{6,5},{7,6},{8,7},{9,8},{10,9},{11,1... | collective-permute-start | bytes 61448 | tf_op jit(solution)/shard_map/ppermute | solution.py:330
  28.8 12.2 %collective-permute-start.3 = (bf16[8,128]{1,0:T(8,128)(2,1)S(1)}, bf16[8,128]{1,0:T(8,128)(2,1)S(1)}, u32[]{:S(2)}, u32[]{:S(2)}) collective-permute-start(bf16[8,128]{1,0:T(8,128)(2,1)S(1)} %convert.39), channel_id=1, source_target_pairs={{0,1},{1,2},{2,3},{3,4},{4,5},{5,6},{6,7},{7,8},{8,9},{9,10},{10,1... | collective-permute-start | bytes 6152 | tf_op jit(solution)/shard_map/ppermute | solution.py:331
  42.1 17.3 %all-to-all-start.1 = ((bf16[16,16,128]{2,1,0:T(8,128)(2,1)}), bf16[16,16,128]{2,1,0:T(8,128)(2,1)S(1)}, u32[]{:S(2)}, u32[]{:S(2)}) async-start(bf16[16,16,128]{2,1,0:T(8,128)(2,1)} %broadcast_in_dim.38), calls=%async_computation.1 | async-start | bytes 131072 | tf_op jit(solution)/shard_map/all_to_all | solution.py:358
  53.8 10.6 %collective-permute-start.4 = (bf16[32,4352]{1,0:T(8,128)(2,1)S(1)}, bf16[32,4352]{1,0:T(8,128)(2,1)S(1)}, u32[]{:S(2)}, u32[]{:S(2)}) collective-permute-start(bf16[32,4352]{1,0:T(8,128)(2,1)S(1)} %reshape.89.sown_ref), channel_id=1, source_target_pairs={{0,1},{1,0},{2,3},{3,2},{4,5},{5,4},{6,7},{7,6},{8,9},{9,8},{10,11... | collective-permute-start | bytes 835592 | tf_op jit(solution)/shard_map/ppermute | solution.py:341
  78.5 0.8 copy-start.1
  79.3 11.2 %collective-permute-start.5 = (s16[32,4224]{1,0:T(8,128)(2,1)S(1)}, s16[32,4224]{1,0:T(8,128)(2,1)S(1)}, u32[]{:S(2)}, u32[]{:S(2)}) collective-permute-start(s16[32,4224]{1,0:T(8,128)(2,1)S(1)} %get-tuple-element.32), channel_id=1, source_target_pairs={{0,1},{1,0},{2,3},{3,2},{4,5},{5,4},{6,7},{7,6},{8,9},{9,8},{10,11... | collective-permute-start | bytes 811016 | tf_op jit(solution)/shard_map/ppermute | solution.py:407
  82.7 13.6 %all-to-all-start.3 = ((f32[16,4,256]{2,1,0:T(4,128)}), f32[16,4,256]{2,1,0:T(4,128)S(1)}, u32[]{:S(2)}, u32[]{:S(2)}) async-start(f32[16,4,256]{2,1,0:T(4,128)} %copy.45), calls=%async_computation.3 | async-start | bytes 131072 | tf_op jit(solution)/shard_map/all_to_all | solution.py:409
  90.5 0.7 copy-start.7
